TPU v7x, 256 devices: a whole 4x4x8 slice. The times are simulated.
256 devices in a mesh: sec: 16 (over y, z_hi), dev: 16 (over x, z_lo, core).
Axes of the slice: x: 4, y: 4, z: 8 (z_hi: 4, z_lo: 2; z = z_hi * 2 + z_lo), core: 2. Of those that a mesh axis runs over, the one named last changes fastest.
Arguments:
- velocity: bfloat16 [2, 3, 128, 192, 192], P(None, None, 'sec', 'dev'), may hold values from -6 to 6
- acoustic: float32 [4, 16, 64, 8, 512], P(None, 'sec', 'dev'), may hold values from -6 to 6
- interp: bfloat16 [512, 512], replicated, may hold values from -0.25 to 0.25
- source_peer: int32 [6144, 1], P(('sec', 'dev')), may hold values from 0 to 15; in each aligned block of 24 rows (0 to 23, 24 to 47, ...) at most 3 rows name the same one
- source_block: int32 [6144], P(('sec', 'dev')), may hold values from 0 to 35
- source_element: int32 [6144], P(('sec', 'dev')), may hold values from 0 to 31, as said below
Outputs:
- acoustic_next: float32 [4, 16, 64, 8, 512], P(None, 'sec', 'dev')
- sources: bfloat16 [6144, 2, 3, 512], P(('sec', 'dev'))
Inputs may be any that keep to these rules, and one draw needn't show every extreme that they name: `source_peer`: among the rows of one device no value appears more than 3 times, and some device reaches 3. `source_element`: the 24 entries of one device are distinct.
All inputs are finite; a program needn't handle non-finite values.
Results may differ from a plain program's by a relative error of at most 0.0049.
Values may be sent and summed in bfloat16 or wider, within the bound.
A program may use at most 128 MiB of HBM per device.

v0:
```python
import functools
import jax
import jax.numpy as jnp
import ml_dtypes
import numpy as np
from jax import lax
from jax.experimental import pallas as pl
from jax.experimental.pallas import tpu as pltpu
from jax.sharding import PartitionSpec as P

MESH = pl.DeviceIdType.MESH
F32 = jnp.float32
BF16 = jnp.bfloat16
time_delta = 0.03
lift_half = 14.0
STAGE = (1.0 / 3.0, 0.5, 1.0)
CAP = 3
ROWS = 16


def cheb_matrix():
    points_n = 8
    nodes_at = -np.cos(np.pi * np.arange(points_n) / (points_n - 1))
    weights_at = np.ones(points_n)
    weights_at[0] = 0.5
    weights_at[-1] = 0.5
    weights_at = weights_at * (-1.0) ** np.arange(points_n)
    result_mat = np.zeros((points_n, points_n))
    for row_at in range(points_n):
        for col_at in range(points_n):
            if row_at != col_at:
                result_mat[row_at, col_at] = (
                    weights_at[col_at] / weights_at[row_at] / (nodes_at[row_at] - nodes_at[col_at])
                )
        result_mat[row_at, row_at] = -np.sum(result_mat[row_at])
    return result_mat


def tables():
    own = -cheb_matrix()
    own[7, 7] += lift_half
    own[0, 0] -= lift_half
    eye2, eye8 = np.eye(2), np.eye(8)
    packed = []
    for dense in (np.kron(eye2, np.kron(own, eye8)).T, np.kron(eye2, np.kron(eye8, own)).T):
        high = dense.astype(ml_dtypes.bfloat16)
        low = (dense - high.astype(np.float64)).astype(ml_dtypes.bfloat16)
        packed.append(np.block([[high, low], [high, np.zeros_like(high)]]))
    coef = np.zeros((4, 4, 2, 128), np.float32)
    for out_at in range(4):
        for in_at in range(4):
            for odd in range(2):
                coef[out_at, in_at, odd, :64] = own[2 * out_at, 2 * in_at + odd]
                coef[out_at, in_at, odd, 64:] = own[2 * out_at + 1, 2 * in_at + odd]
    return np.stack(packed).astype(ml_dtypes.bfloat16), coef.reshape(32, 128)


def roll(values, shift, axis):
    size = values.shape[axis]
    return pltpu.roll(values, shift % size, axis)


def lane_iota(shape):
    return lax.broadcasted_iota(jnp.int32, shape, len(shape) - 1)


def kernel(
    n_sec, n_dev,
    vel, ac, interp, peer, block, elem, wtab, coef,
    out_q, out_s,
    velb, acv, ip, wv, vs, lr, yhs, xhr, yhr, idx_src, idx_buf, sendb, recvb, yy_ref, forc,
    fxs, fxr, fys, fyr, dgs, dgr,
    local_sem, hx_s, hx_r, hy_s, hy_r, id_s, id_r, aa_s, aa_r, fx_s, fx_r, fy_s, fy_r, dg_s, dg_r,
):
    sec = lax.axis_index("sec")
    dev = lax.axis_index("dev")
    has_x = (sec > 0, sec < n_sec - 1)
    has_y = (dev > 0, dev < n_dev - 1)
    x_at = (sec - 1, sec + 1)
    y_at = (dev - 1, dev + 1)

    def dev_of(offset):
        return lax.rem(dev + offset + n_dev, n_dev)

    for ref in (xhr, yhr, fxr, fyr, dgr):
        ref[...] = jnp.zeros(ref.shape, ref.dtype)

    barrier = pltpu.get_barrier_semaphore()
    for side in range(2):
        @pl.when(has_x[side])
        def _():
            pl.semaphore_signal(barrier, inc=1, device_id=(x_at[side], dev), device_id_type=MESH)

    def greet(offset, carry):
        pl.semaphore_signal(barrier, inc=1, device_id=(sec, dev_of(offset)), device_id_type=MESH)
        return carry

    lax.fori_loop(1, n_dev, greet, 0)

    loads = [
        pltpu.make_async_copy(vel, velb, local_sem.at[0]),
        pltpu.make_async_copy(ac, acv, local_sem.at[1]),
        pltpu.make_async_copy(wtab, wv, local_sem.at[2]),
    ] + [pltpu.make_async_copy(interp.at[:, at], ip.at[at], local_sem.at[3 + at]) for at in range(4)]
    for load in loads:
        load.start()

    vs[...] = jnp.zeros(vs.shape, F32)
    lr[...] = jnp.zeros(lr.shape, F32)

    count = peer.shape[0]
    row_k = lax.broadcasted_iota(jnp.int32, (count, 128), 0)
    col_k = lax.broadcasted_iota(jnp.int32, (count, 128), 1)
    peer_col = peer[...].astype(F32)
    peer_row = jnp.sum(jnp.where(row_k == col_k, peer_col, 0.0), axis=0, keepdims=True)
    same = (peer_row == peer_col) & (col_k < count)
    rank_col = jnp.sum(jnp.where(same & (col_k < row_k), 1.0, 0.0), axis=1, keepdims=True)
    rank_row = jnp.sum(jnp.where(same & (row_k < col_k), 1.0, 0.0), axis=0, keepdims=True)
    lane = lane_iota((1, 128))
    idx_src[0:1, :] = jnp.where(lane < count, peer_row * CAP + rank_row, -1.0)
    idx_src[1:2, :] = jnp.zeros((1, 128), F32)
    idx_src[1:2, 0:count] = block[...].astype(F32)
    key_col = peer_col * ROWS + rank_col * CAP
    key_row = peer_row * ROWS + rank_row * CAP
    idx_buf[pl.ds(dev, 1)] = idx_src[...][None]

    loads[0].wait()
    for t in range(2):
        for side, at in ((0, 11), (1, 0)):
            for slot, comp in enumerate((0, 2)):
                yhs[t, side, slot * 8:slot * 8 + 8, :] = velb[t, comp, :, at, :]
    loads[1].wait()
    for field in range(4):
        for part in range(4):
            yy_ref[0, field, part] = acv[field, :, part * 128:(part + 1) * 128]

    def put_faces(k):
        p, u1, u2 = yy_ref.at[k, 0], yy_ref.at[k, 1], yy_ref.at[k, 2]
        fxs[k, 0] = (u1[3] + p[3]).astype(BF16)
        fxs[k, 1] = (u1[0] - p[0]).astype(BF16)
        fys[k, 0] = (u2[:, 24:32] + p[:, 24:32]).reshape(32, 128).astype(BF16)
        fys[k, 1] = (u2[:, 0:8] - p[:, 0:8]).reshape(32, 128).astype(BF16)

    def x_copy(k, way, to):
        return pltpu.make_async_remote_copy(
            fxs.at[k, way], fxr.at[k, way], fx_s.at[k, way], fx_r.at[k, way],
            device_id=(to, dev), device_id_type=MESH)

    def y_copy(k, way, to):
        return pltpu.make_async_remote_copy(
            fys.at[k, way], fyr.at[k, way], fy_s.at[k, way], fy_r.at[k, way],
            device_id=(sec, to), device_id_type=MESH)

    def send_faces(k):
        for way in range(2):
            @pl.when(has_x[1 - way])
            def _():
                x_copy(k, way, x_at[1 - way]).start()
        for way in range(2):
            @pl.when(has_y[1 - way])
            def _():
                y_copy(k, way, y_at[1 - way]).start()

    def take_faces(k):
        for way in range(2):
            @pl.when(has_y[way])
            def _():
                y_copy(k, way, y_at[way]).wait_recv()
        for way in range(2):
            @pl.when(has_x[way])
            def _():
                x_copy(k, way, x_at[way]).wait_recv()

    def diagonal(k, way, to_x, to_y):
        return pltpu.make_async_remote_copy(
            dgs.at[k - 1, way], dgr.at[k - 1, way], dg_s.at[k - 1, way], dg_r.at[k - 1, way],
            device_id=(to_x, to_y), device_id_type=MESH)

    corners = ((0, 0), (1, 0), (0, 1), (1, 1))

    def send_edges(k):
        p, u1, u2 = yy_ref.at[k, 0], yy_ref.at[k, 1], yy_ref.at[k, 2]
        for at, (way_x, way_y) in enumerate(corners):
            part = 3 if way_x == 0 else 0
            rows = slice(24, 32) if way_y == 0 else slice(0, 8)
            pp = p[part, rows]
            first = u1[part, rows] + (pp if way_x == 0 else -pp)
            second = u2[part, rows] + (pp if way_y == 0 else -pp)
            dgs[k - 1, at] = jnp.concatenate([first, second], axis=0).astype(BF16)
        for at, (way_x, way_y) in enumerate(corners):
            @pl.when(has_x[1 - way_x] & has_y[1 - way_y])
            def _():
                diagonal(k, at, x_at[1 - way_x], y_at[1 - way_y]).start()

    def take_edges(k):
        for at, (way_x, way_y) in enumerate(corners):
            @pl.when(has_x[way_x] & has_y[way_y])
            def _():
                diagonal(k, at, x_at[way_x], y_at[way_y]).wait_recv()

    def hx_copy(t, way, to):
        return pltpu.make_async_remote_copy(
            vel.at[t, 1:3, 7 if way == 0 else 0], xhr.at[t, way], hx_s.at[t, way], hx_r.at[t, way],
            device_id=(to, dev), device_id_type=MESH)

    def hy_copy(t, way, to):
        return pltpu.make_async_remote_copy(
            yhs.at[t, way], yhr.at[t, way], hy_s.at[t, way], hy_r.at[t, way],
            device_id=(sec, to), device_id_type=MESH)

    def id_copy(offset, slot, to):
        return pltpu.make_async_remote_copy(
            idx_src, idx_buf.at[slot], id_s.at[offset], id_r.at[offset],
            device_id=(sec, to), device_id_type=MESH)

    def aa_copy(t, offset, slot, to):
        return pltpu.make_async_remote_copy(
            sendb.at[t, to], recvb.at[t, slot], aa_s.at[t, offset], aa_r.at[t, offset],
            device_id=(sec, to), device_id_type=MESH)

    def each_peer(action):
        def step(offset, carry):
            action(offset)
            return carry
        lax.fori_loop(1, n_dev, step, 0)

    put_faces(0)
    greeted = n_dev - 1 + has_x[0].astype(jnp.int32) + has_x[1].astype(jnp.int32)
    pl.semaphore_wait(barrier, greeted)

    def send_halo(t):
        for way in range(2):
            @pl.when(has_x[1 - way])
            def _():
                hx_copy(t, way, x_at[1 - way]).start()
        for way in range(2):
            @pl.when(has_y[1 - way])
            def _():
                hy_copy(t, way, y_at[1 - way]).start()

    send_halo(0)
    each_peer(lambda offset: id_copy(offset, dev, dev_of(offset)).start())
    send_halo(1)
    send_faces(0)

    for t in range(2):
        vs[t, :, 1:9, 1:13, 0:192] = velb[t].astype(F32)

    loads[2].wait()
    lanes = lane_iota((1, 1, 128))
    low_half = lanes < 64
    at_b = (lanes >> 3) & 7
    at_c = lanes & 7
    part_at = lax.broadcasted_iota(jnp.int32, (4, 1, 128), 0)
    lane4 = lane_iota((4, 1, 128))
    b4, c4 = (lane4 >> 3) & 7, lane4 & 7

    def on(flag):
        return jnp.where(flag, -lift_half, 0.0)

    on_x = on(((part_at == 0) & (lane4 < 64)) | ((part_at == 3) & (lane4 >= 64)))
    on_y = on((b4 == 0) | (b4 == 7))
    on_z = on((c4 == 0) | (c4 == 7))
    on_all = on_x + on_y + on_z
    ez = lax.broadcasted_iota(jnp.int32, (1, 32, 1), 1) & 7

    def along_first(values):
        turned = roll(values, 64, 2)
        even = jnp.where(low_half, values, turned)
        odd = jnp.where(low_half, turned, values)
        parts = []
        for out_at in range(4):
            total = None
            for in_at in range(4):
                row = (out_at * 4 + in_at) * 2
                term = even[in_at] * coef[row:row + 1, :] + odd[in_at] * coef[row + 1:row + 2, :]
                total = term if total is None else total + term
            parts.append(total)
        return jnp.stack(parts)

    def along_lanes(first, second, which):
        flat = jnp.concatenate([first, second], axis=0).reshape(256, 128)
        high = flat.astype(BF16)
        rest = (flat - high.astype(F32)).astype(BF16)
        both = jnp.dot(jnp.concatenate([high, rest], axis=1), wv[which], preferred_element_type=F32)
        both = (both[:, :128] + both[:, 128:]).reshape(8, 32, 128)
        return both[:4], both[4:]

    def local_rate(k):
        p, u1, u2, u3 = (yy_ref[k, field] for field in range(4))
        dp2, du2 = along_lanes(p, u2, 0)
        dp3, du3 = along_lanes(p, u3, 1)
        r1 = along_first(p) + on_x * u1
        rp = along_first(u1) + on_all * p + du2 + du3
        r2 = dp2 + on_y * u2
        r3 = dp3 + on_z * u3
        none = jnp.zeros((4, 8, 128), F32)
        out2, back2 = u2 + p, u2 - p
        from_low = jnp.where(at_b == 0, roll(jnp.concatenate([none, out2[:, :24]], axis=1), -56, 2), 0.0)
        from_high = jnp.where(at_b == 7, roll(jnp.concatenate([back2[:, 8:], none], axis=1), 56, 2), 0.0)
        out3, back3 = u3 + p, u3 - p
        lower = roll(roll(out3, 1, 1), -7, 2)
        upper = roll(roll(back3, -1, 1), 7, 2)
        below = jnp.where((at_c == 0) & (ez > 0), lower, 0.0)
        above = jnp.where((at_c == 7) & (ez < 7), upper, 0.0)
        rp = rp + lift_half * ((from_low - from_high) + (below - above))
        r2 = r2 + lift_half * (from_low + from_high)
        r3 = r3 + lift_half * (below + above)
        return rp, r1, r2, r3

    def advance_local(k, start, force):
        scale = STAGE[k % 3] * time_delta
        rates = local_rate(k)
        for field in range(4):
            rate = rates[field]
            if force is not None and field:
                rate = rate + forc[force, field - 1]
            yy_ref[k + 1, field] = yy_ref[start, field] + scale * rate

    wide = lane_iota((8, 128))

    def between(first, last):
        return (wide >= first) & (wide < last)

    def add_neighbours(k, corrected):
        amount = STAGE[k % 3] * time_delta * lift_half
        x_low, x_high = fxr[k, 0].astype(F32), fxr[k, 1].astype(F32)
        y_low = fyr[k, 0].astype(F32).reshape(4, 8, 128)
        y_high = fyr[k, 1].astype(F32).reshape(4, 8, 128)
        if corrected:
            before = STAGE[(k - 1) % 3] * time_delta * lift_half
            edges = [dgr[k - 2, at].astype(F32) * before for at in range(4)]
            ex = [edge[0:8] for edge in edges]
            ey = [edge[8:16] for edge in edges]

            def moved(values, shift, first, last):
                return jnp.where(between(first, last), roll(values, shift, 1), 0.0)

            none = jnp.zeros((16, 128), F32)
            x_low = x_low + jnp.concatenate(
                [moved(ey[0], -56, 64, 72), none, -moved(ey[2], 56, 120, 128)], axis=0)
            x_high = x_high + jnp.concatenate(
                [-moved(ey[1], -56, 0, 8), none, moved(ey[3], 56, 56, 64)], axis=0)
            nil = jnp.zeros((8, 128), F32)
            y_low = y_low + jnp.stack(
                [moved(ex[0], 64, 56, 64), nil, nil, -moved(ex[1], 64, 120, 128)])
            y_high = y_high + jnp.stack(
                [-moved(ex[2], 64, 0, 8), nil, nil, moved(ex[3], 64, 64, 72)])
        half = lane_iota((32, 128)) < 64
        x_low = amount * jnp.where(half, roll(x_low, 64, 1), 0.0)
        x_high = amount * jnp.where(half, 0.0, roll(x_high, 64, 1))
        y_low = amount * jnp.where(at_b == 0, roll(y_low, -56, 2), 0.0)
        y_high = amount * jnp.where(at_b == 7, roll(y_high, 56, 2), 0.0)
        to = k + 1
        yy_ref[to, 0, 0] += x_low
        yy_ref[to, 1, 0] += x_low
        yy_ref[to, 0, 3] -= x_high
        yy_ref[to, 1, 3] += x_high
        yy_ref[to, 0, :, 0:8] += y_low
        yy_ref[to, 2, :, 0:8] += y_low
        yy_ref[to, 0, :, 24:32] -= y_high
        yy_ref[to, 2, :, 24:32] += y_high

    advance_local(0, 0, None)

    each_peer(lambda offset: id_copy(offset, dev_of(-offset), dev_of(-offset)).wait_recv())
    row_r = lax.broadcasted_iota(jnp.int32, (1, ROWS, 1), 1)
    slot_j = jnp.where(row_r >= 3, 1, 0) + jnp.where(row_r >= 6, 1, 0)
    comp_c = row_r - 3 * slot_j
    wanted = jnp.where(row_r < 9, CAP * dev + slot_j, -7).astype(F32)
    codes = jnp.broadcast_to(idx_buf[:, 0:1, :], (n_dev, ROWS, 128))
    names = jnp.broadcast_to(idx_buf[:, 1:2, :], (n_dev, ROWS, 128))
    found = jnp.sum(jnp.where(codes == wanted, names + 1.0, 0.0), axis=2, keepdims=True)
    name = found - 1.0
    name_y = jnp.where(name >= 12.0, 1.0, 0.0) + jnp.where(name >= 24.0, 1.0, 0.0)
    target = (name - 12.0 * name_y) * 16.0 + comp_c.astype(F32) * 3.0 + name_y
    target = jnp.where(found > 0.0, target, -1.0).reshape(n_dev * ROWS, 1)
    pick = jnp.where(lane_iota((n_dev * ROWS, 192)).astype(F32) == target, 1.0, 0.0).astype(BF16)

    in_row = lane_iota((32, n_dev * ROWS)).astype(F32)
    rows_e = lax.broadcasted_iota(jnp.int32, (32, count), 0)
    hit = rows_e == elem[...]
    key_e = jnp.sum(jnp.where(hit, key_row[:, 0:count] + 1.0, 0.0), axis=1, keepdims=True)
    place = jnp.concatenate(
        [jnp.where((in_row == key_e - 1.0 + c) & (key_e > 0.0), 1.0, 0.0) for c in range(3)],
        axis=0).astype(BF16)
    in_row_k = lane_iota((count, n_dev * ROWS)).astype(F32)
    choose = jnp.concatenate(
        [jnp.where(in_row_k == key_col + c, 1.0, 0.0) for c in range(3)], axis=0).astype(BF16)

    def swap_chunks(values):
        chunk = lane_iota((1, 1, 1, 128)) >> 4
        for bit in range(3):
            step = 1 << bit
            pairs = values.reshape(4 >> bit, 2, step, 16, 128)
            first = pairs[:, 0].reshape(4, 16, 128)
            second = pairs[:, 1].reshape(4, 16, 128)
            upper = (chunk[0] >> bit) & 1 == 1
            new_first = jnp.where(upper, roll(second, 16 * step, 2), first)
            new_second = jnp.where(upper, second, roll(first, -16 * step, 2))
            shape = (4 >> bit, 1, step, 16, 128)
            values = jnp.concatenate(
                [new_first.reshape(shape), new_second.reshape(shape)], axis=1).reshape(8, 16, 128)
        return values

    def lamb_sources(t):
        for way in range(2):
            @pl.when(has_y[way])
            def _():
                hy_copy(t, way, y_at[way]).wait_recv()
        for way in range(2):
            @pl.when(has_x[way])
            def _():
                hx_copy(t, way, x_at[way]).wait_recv()
        for way, at in ((0, 0), (1, 9)):
            vs[t, 1:3, at, 1:13, 0:192] = xhr[t, way].astype(F32)
        for way, at in ((0, 0), (1, 13)):
            for slot, comp in enumerate((0, 2)):
                vs[t, comp, 1:9, at, 0:192] = yhr[t, way, slot * 8:slot * 8 + 8, :].astype(F32)

        def cells(comp, dx, dy):
            return vs[t, comp, 1 + dx:9 + dx, 1 + dy:17 + dy, :]

        def slope_x(comp):
            return (cells(comp, 1, 0) - cells(comp, -1, 0)) * 0.5

        def slope_y(comp):
            return (cells(comp, 0, 1) - cells(comp, 0, -1)) * 0.5

        def slope_z(comp):
            here = cells(comp, 0, 0)
            return (roll(here, -1, 2) - roll(here, 1, 2)) * 0.5

        curl_x = slope_y(2) - slope_z(1)
        curl_y = slope_z(0) - slope_x(2)
        curl_z = slope_x(1) - slope_y(0)
        v_x, v_y, v_z = cells(0, 0, 0), cells(1, 0, 0), cells(2, 0, 0)
        lamb = (curl_y * v_z - curl_z * v_y, curl_z * v_x - curl_x * v_z, curl_x * v_y - curl_y * v_x)
        for comp in range(3):
            for side in range(2):
                lr[side, :, comp * 12:comp * 12 + 12, :] = lamb[comp][:, :12, side * 128:side * 128 + 128]
        columns = []
        for row in range(4):
            low = swap_chunks(lr[0, :, pl.ds(row, 16, stride=4), :])
            high = swap_chunks(lr[1, :, pl.ds(row, 16, stride=4), :])
            columns.append(jnp.concatenate([low, high[:4]], axis=0))
        cut = jnp.concatenate(columns, axis=2).reshape(192, 512).astype(BF16)
        made = jnp.dot(cut, ip[...].reshape(512, 512), preferred_element_type=F32).astype(BF16)
        sent = jnp.dot(pick, made, preferred_element_type=F32).astype(BF16)
        sendb[t] = sent.reshape(n_dev, ROWS, 512)
        recvb[t, pl.ds(dev, 1)] = sendb[t, pl.ds(dev, 1)]

    def put_forcing(t):
        table = recvb[t].reshape(n_dev * ROWS, 512)
        placed = jnp.dot(place, table, preferred_element_type=F32)
        for comp in range(3):
            for part in range(4):
                forc[t, comp, part] = placed[comp * 32:comp * 32 + 32, part * 128:part * 128 + 128]

    def put_sources(t):
        table = recvb[t].reshape(n_dev * ROWS, 512)
        chosen = jnp.dot(choose, table, preferred_element_type=F32).astype(BF16)
        for comp in range(3):
            out_s[t * 3 + comp] = chosen[comp * count:comp * count + count]

    for at in range(4):
        loads[3 + at].wait()
    lamb_sources(0)
    each_peer(lambda offset: aa_copy(0, offset, dev, dev_of(offset)).start())
    take_faces(0)
    add_neighbours(0, False)
    lamb_sources(1)
    each_peer(lambda offset: aa_copy(0, offset, dev_of(-offset), dev_of(-offset)).wait_recv())
    put_forcing(0)
    for field in range(3):
        yy_ref[1, 1 + field] += (STAGE[0] * time_delta) * forc[0, field]
    put_faces(1)
    send_faces(1)
    send_edges(1)
    each_peer(lambda offset: aa_copy(1, offset, dev, dev_of(offset)).start())

    advance_local(1, 0, 0)
    put_faces(2)
    send_faces(2)
    put_sources(0)
    take_faces(1)
    add_neighbours(1, False)
    send_edges(2)

    advance_local(2, 0, 0)
    put_faces(3)
    send_faces(3)
    take_faces(2)
    take_edges(1)
    add_neighbours(2, True)
    send_edges(3)

    each_peer(lambda offset: aa_copy(1, offset, dev_of(-offset), dev_of(-offset)).wait_recv())
    put_forcing(1)
    advance_local(3, 3, 1)
    put_faces(4)
    send_faces(4)
    put_sources(1)
    take_faces(3)
    take_edges(2)
    add_neighbours(3, True)
    send_edges(4)

    advance_local(4, 3, 1)
    put_faces(5)
    send_faces(5)
    take_faces(4)
    take_edges(3)
    add_neighbours(4, True)

    advance_local(5, 3, 1)
    take_faces(5)
    take_edges(4)
    add_neighbours(5, True)
    for field in range(4):
        for part in range(4):
            out_q[field, :, part * 128:(part + 1) * 128] = yy_ref[6, field, part]

    for t in range(2):
        for way in range(2):
            @pl.when(has_x[1 - way])
            def _():
                hx_copy(t, way, x_at[1 - way]).wait_send()

            @pl.when(has_y[1 - way])
            def _():
                hy_copy(t, way, y_at[1 - way]).wait_send()
        each_peer(lambda offset: aa_copy(t, offset, dev, dev_of(offset)).wait_send())
    each_peer(lambda offset: id_copy(offset, dev, dev_of(offset)).wait_send())
    for k in range(6):
        for way in range(2):
            @pl.when(has_x[1 - way])
            def _():
                x_copy(k, way, x_at[1 - way]).wait_send()

            @pl.when(has_y[1 - way])
            def _():
                y_copy(k, way, y_at[1 - way]).wait_send()
    for k in range(1, 5):
        for at, (way_x, way_y) in enumerate(corners):
            @pl.when(has_x[1 - way_x] & has_y[1 - way_y])
            def _():
                diagonal(k, at, x_at[1 - way_x], y_at[1 - way_y]).wait_send()


def body(n_sec, n_dev, velocity, acoustic, interp, source_peer, source_block, source_element):
    count = source_peer.shape[0]
    wtab, coef = tables()
    any_spec = pl.BlockSpec(memory_space=pltpu.HBM)
    vmem = pl.BlockSpec(memory_space=pltpu.VMEM)
    dma = pltpu.SemaphoreType.DMA
    acoustic_next, sources = pl.pallas_call(
        functools.partial(kernel, n_sec, n_dev),
        out_shape=(
            jax.ShapeDtypeStruct((4, 32, 512), F32),
            jax.ShapeDtypeStruct((6, count, 512), BF16),
        ),
        in_specs=[any_spec, any_spec, any_spec, vmem, vmem, vmem, any_spec, vmem],
        out_specs=(vmem, vmem),
        scratch_shapes=[
            pltpu.VMEM((2, 3, 8, 12, 192), BF16),
            pltpu.VMEM((4, 32, 512), F32),
            pltpu.VMEM((4, 8, 16, 512), BF16),
            pltpu.VMEM((2, 256, 256), BF16),
            pltpu.VMEM((2, 3, 10, 24, 256), F32),
            pltpu.VMEM((2, 8, 64, 128), F32),
            pltpu.VMEM((2, 2, 16, 192), BF16),
            pltpu.VMEM((2, 2, 2, 12, 192), BF16),
            pltpu.VMEM((2, 2, 16, 192), BF16),
            pltpu.VMEM((2, 128), F32),
            pltpu.VMEM((n_dev, 2, 128), F32),
            pltpu.VMEM((2, n_dev, ROWS, 512), BF16),
            pltpu.VMEM((2, n_dev, ROWS, 512), BF16),
            pltpu.VMEM((7, 4, 4, 32, 128), F32),
            pltpu.VMEM((2, 3, 4, 32, 128), F32),
            pltpu.VMEM((6, 2, 32, 128), BF16),
            pltpu.VMEM((6, 2, 32, 128), BF16),
            pltpu.VMEM((6, 2, 32, 128), BF16),
            pltpu.VMEM((6, 2, 32, 128), BF16),
            pltpu.VMEM((4, 4, 16, 128), BF16),
            pltpu.VMEM((4, 4, 16, 128), BF16),
            dma((7,)),
            dma((2, 2)), dma((2, 2)), dma((2, 2)), dma((2, 2)),
            dma((n_dev,)), dma((n_dev,)),
            dma((2, n_dev)), dma((2, n_dev)),
            dma((6, 2)), dma((6, 2)), dma((6, 2)), dma((6, 2)),
            dma((4, 4)), dma((4, 4)),
        ],
        compiler_params=pltpu.CompilerParams(
            collective_id=0, has_side_effects=True, vmem_limit_bytes=40 * 1024 * 1024),
    )(
        velocity,
        acoustic.reshape(4, 32, 512),
        interp.reshape(8, 4, 16, 512),
        source_peer,
        source_block.reshape(1, count),
        source_element.reshape(1, count),
        jnp.asarray(wtab),
        jnp.asarray(coef),
    )
    sources = sources.reshape(2, 3, count, 512).transpose(2, 0, 1, 3)
    return acoustic_next.reshape(acoustic.shape), sources


def solution(mesh):
    return jax.shard_map(
        functools.partial(body, mesh.shape["sec"], mesh.shape["dev"]),
        mesh=mesh,
        in_specs=(
            P(None, None, "sec", "dev", None),
            P(None, "sec", "dev", None, None),
            P(),
            P(("sec", "dev"), None),
            P(("sec", "dev")),
            P(("sec", "dev")),
        ),
        out_specs=(P(None, "sec", "dev", None, None), P(("sec", "dev"), None, None, None)),
        check_vma=False,
    )
```

profile of v0, /device:TPU:1, one launch (start us, length us, event | category | flops | bytes accessed | tf_op | source)
XLA Modules:
  0.0 41.0 jit_solution(5383245641610807974)
XLA Ops:
  0.6 0.0 copy-start
  0.6 0.8 %copy.11.peer = s32[24,1]{1,0:T(8,128)S(1)} copy(s32[24,1]{0,1:T(1,128)} %param.11) | data formatting | bytes 192 | tf_op args[3]
  1.4 0.0 copy-start.3
  1.4 0.0 copy-start.4
  1.4 0.0 copy-start.5
  1.4 1.1 %copy.10.vel = bf16[2,3,8,12,192]{4,3,2,1,0:T(8,128)(2,1)S(1)} copy(bf16[2,3,8,12,192]{4,2,3,1,0:T(8,128)(2,1)} %param.8) | data formatting | bytes 442368 | tf_op args[0]
  2.5 0.0 copy-done
  2.5 0.0 copy-done.3
  2.5 0.0 copy-done.4
  2.5 0.0 copy-done.5
  2.5 0.0 copy-start.1
  2.6 0.9 %copy-done.1 = f32[4,1,4,8,512]{4,3,2,1,0:T(8,128)S(1)} copy-done((f32[4,1,4,8,512]{4,3,2,1,0:T(8,128)S(1)}, f32[4,1,4,8,512]{4,3,2,1,0:T(8,128)}, u32[]{:S(2)}) %copy-start.1) | copy-done | bytes 262168
  3.5 0.0 copy-start.2
  3.5 0.9 %copy-done.2 = bf16[2,256,256]{2,1,0:T(8,128)(2,1)S(1)} copy-done((bf16[2,256,256]{2,1,0:T(8,128)(2,1)S(1)}, bf16[2,256,256]{2,1,0:T(8,128)(2,1)}, u32[]{:S(2)}) %copy-start.2) | copy-done | bytes 262168
  4.5 35.1 %shard_map.95 = (f32[4,32,512]{2,1,0:T(8,128)S(1)}, bf16[6,24,512]{2,1,0:T(8,128)(2,1)S(1)}) custom-call(bf16[2,3,8,12,192]{4,3,2,1,0:T(8,128)(2,1)S(1)} %copy.10.vel, f32[4,32,512]{2,1,0:T(8,128)S(1)} %bitcast.12, bf16[8,4,16,512]{3,2,1,0:T(8,128)(2,1)S(1)} %bitcast.11, s32[24,1]{1,0:T(8,128)S(1)} %copy.11.peer, s32[1,24]{1,0:T(1,128)S(1)} %bitcast.15, ...), custom_call_target="tpu_custom_call" | custom-call | tf_op jit(solution)/shard_map/pallas_call | solution.py:557
  39.5 0.8 %copy.15 = bf16[2,3,24,512]{3,0,1,2:T(2,128)(2,1)} copy(bf16[2,3,24,512]{3,2,1,0:T(8,128)(2,1)S(1)} %bitcast.14) | data formatting | bytes 294912 | tf_op jit(solution)/shard_map/reshape | solution.py:606
  40.3 0.7 %copy.17 = f32[4,1,4,8,512]{4,3,2,1,0:T(8,128)} copy(f32[4,1,4,8,512]{4,3,2,1,0:T(8,128)S(1)} %bitcast.13) | data formatting | bytes 524288
Async XLA Ops:
  0.6 1.9 %copy-start = (bf16[512,512]{1,0:T(8,128)(2,1)S(1)}, bf16[512,512]{1,0:T(8,128)(2,1)}, u32[]{:S(2)}) copy-start(bf16[512,512]{1,0:T(8,128)(2,1)} %param.10) | copy-start | bytes 1572868
  1.4 1.1 %copy-start.3 = (f32[32,128]{1,0:T(8,128)S(1)}, f32[32,128]{1,0:T(8,128)}, u32[]{:S(2)}) copy-start(f32[32,128]{1,0:T(8,128)} %constant.5.clone.coef) | copy-start | bytes 49156
  1.4 1.1 %copy-start.4 = (s32[24]{0:T(128)S(1)}, s32[24]{0:T(128)}, u32[]{:S(2)}) copy-start(s32[24]{0:T(128)} %param.12) | copy-start | bytes 292
  1.4 1.1 %copy-start.5 = (s32[24]{0:T(128)S(1)}, s32[24]{0:T(128)}, u32[]{:S(2)}) copy-start(s32[24]{0:T(128)} %param.13) | copy-start | bytes 292
  2.5 1.0 %copy-start.1 = (f32[4,1,4,8,512]{4,3,2,1,0:T(8,128)S(1)}, f32[4,1,4,8,512]{4,3,2,1,0:T(8,128)}, u32[]{:S(2)}) copy-start(f32[4,1,4,8,512]{4,3,2,1,0:T(8,128)} %param.9) | copy-start | bytes 786436
  3.5 0.9 %copy-start.2 = (bf16[2,256,256]{2,1,0:T(8,128)(2,1)S(1)}, bf16[2,256,256]{2,1,0:T(8,128)(2,1)}, u32[]{:S(2)}) copy-start(bf16[2,256,256]{2,1,0:T(8,128)(2,1)} %constant.4.clone.wtab) | copy-start | bytes 786436
where the time goes:
time: 41.2 us; the launch traced here: 41 us
  Pallas kernels  35.1 us (85%)
  local copies, waits for them, and re-layouts  5.24 us (13%)
  between operations  0.69 us (2%)
    pallas_call x1, Pallas kernels, body(): pl.pallas_call(functools.partial(kernel, n_sec, n_dev), out_shape=(jax.Sh...  35.1 us
    unnamed x15, local copies, waits for them, and re-layouts  4.47 us

commit v1 on v0

--- a/solution.py
+++ b/solution.py
@@ -66,9 +66,9 @@
 
 def kernel(
     n_sec, n_dev,
-    vel, ac, interp, peer, block, elem, wtab, coef,
+    vel, ac, interp, peer_in, block_in, elem_in, wtab, coef_in,
     out_q, out_s,
-    velb, acv, ip, wv, vs, lr, yhs, xhr, yhr, idx_src, idx_buf, sendb, recvb, yy_ref, forc,
+    velb, acv, ip, wv, coef, peer, block, elem, vs, xs, lr, xhs, xhr, yhr, idx_src, idx_buf, sendb, recvb, yy_ref, forc,
     fxs, fxr, fys, fyr, dgs, dgr,
     local_sem, hx_s, hx_r, hy_s, hy_r, id_s, id_r, aa_s, aa_r, fx_s, fx_r, fy_s, fy_r, dg_s, dg_r,
 ):
@@ -101,17 +101,29 @@
         pltpu.make_async_copy(vel, velb, local_sem.at[0]),
         pltpu.make_async_copy(ac, acv, local_sem.at[1]),
         pltpu.make_async_copy(wtab, wv, local_sem.at[2]),
-    ] + [pltpu.make_async_copy(interp.at[:, at], ip.at[at], local_sem.at[3 + at]) for at in range(4)]
-    for load in loads:
-        load.start()
+    ] + [pltpu.make_async_copy(interp.at[:, at], ip.at[at], local_sem.at[3 + at]) for at in range(4)] + [
+        pltpu.make_async_copy(coef_in, coef, local_sem.at[7]),
+        pltpu.make_async_copy(peer_in, peer, local_sem.at[8]),
+        pltpu.make_async_copy(block_in, block, local_sem.at[9]),
+        pltpu.make_async_copy(elem_in, elem, local_sem.at[10]),
+    ]
+    for at in (0, 8, 9, 10, 1, 2, 7, 3, 4, 5, 6):
+        loads[at].start()
 
     vs[...] = jnp.zeros(vs.shape, F32)
-    lr[...] = jnp.zeros(lr.shape, F32)
-
-    count = peer.shape[0]
+    xs[...] = jnp.zeros(xs.shape, F32)
+    lr[:, 288:512, :] = jnp.zeros((2, 224, 128), F32)
+
+    for at in (8, 9, 10):
+        loads[at].wait()
+    count = peer.shape[1]
     row_k = lax.broadcasted_iota(jnp.int32, (count, 128), 0)
     col_k = lax.broadcasted_iota(jnp.int32, (count, 128), 1)
-    peer_col = peer[...].astype(F32)
+    square = (count, count)
+    row_s = lax.broadcasted_iota(jnp.int32, square, 0)
+    col_s = lax.broadcasted_iota(jnp.int32, square, 1)
+    peer_col = jnp.sum(
+        jnp.where(row_s == col_s, peer[...].astype(F32), 0.0), axis=1, keepdims=True)
     peer_row = jnp.sum(jnp.where(row_k == col_k, peer_col, 0.0), axis=0, keepdims=True)
     same = (peer_row == peer_col) & (col_k < count)
     rank_col = jnp.sum(jnp.where(same & (col_k < row_k), 1.0, 0.0), axis=1, keepdims=True)
@@ -126,9 +138,10 @@
 
     loads[0].wait()
     for t in range(2):
-        for side, at in ((0, 11), (1, 0)):
-            for slot, comp in enumerate((0, 2)):
-                yhs[t, side, slot * 8:slot * 8 + 8, :] = velb[t, comp, :, at, :]
+        for comp in (1, 2):
+            own = velb[t, comp].astype(F32)
+            for side, at in ((0, 7), (1, 0)):
+                xhs[t, side, comp - 1] = own[:, at, :].astype(BF16)
     loads[1].wait()
     for field in range(4):
         for part in range(4):
@@ -200,12 +213,12 @@
 
     def hx_copy(t, way, to):
         return pltpu.make_async_remote_copy(
-            vel.at[t, 1:3, 7 if way == 0 else 0], xhr.at[t, way], hx_s.at[t, way], hx_r.at[t, way],
+            xhs.at[t, way], xhr.at[t, way], hx_s.at[t, way], hx_r.at[t, way],
             device_id=(to, dev), device_id_type=MESH)
 
     def hy_copy(t, way, to):
         return pltpu.make_async_remote_copy(
-            yhs.at[t, way], yhr.at[t, way], hy_s.at[t, way], hy_r.at[t, way],
+            vel.at[t, :, 11 if way == 0 else 0], yhr.at[t, way], hy_s.at[t, way], hy_r.at[t, way],
             device_id=(sec, to), device_id_type=MESH)
 
     def id_copy(offset, slot, to):
@@ -244,9 +257,10 @@
     send_faces(0)
 
     for t in range(2):
-        vs[t, :, 1:9, 1:13, 0:192] = velb[t].astype(F32)
+        vs[t, :, 1:13, :, 0:192] = velb[t].astype(F32)
 
     loads[2].wait()
+    loads[7].wait()
     lanes = lane_iota((1, 1, 128))
     low_half = lanes < 64
     at_b = (lanes >> 3) & 7
@@ -412,37 +426,43 @@
             @pl.when(has_x[way])
             def _():
                 hx_copy(t, way, x_at[way]).wait_recv()
-        for way, at in ((0, 0), (1, 9)):
-            vs[t, 1:3, at, 1:13, 0:192] = xhr[t, way].astype(F32)
+        for way, at in ((0, 0), (1, 7)):
+            for slot in range(2):
+                xs[t, way, slot, :, at, 0:192] = xhr[t, way, slot].astype(F32)
         for way, at in ((0, 0), (1, 13)):
-            for slot, comp in enumerate((0, 2)):
-                vs[t, comp, 1:9, at, 0:192] = yhr[t, way, slot * 8:slot * 8 + 8, :].astype(F32)
-
-        def cells(comp, dx, dy):
-            return vs[t, comp, 1 + dx:9 + dx, 1 + dy:17 + dy, :]
+            vs[t, :, at, :, 0:192] = yhr[t, way].astype(F32)
+        x_cell = lax.broadcasted_iota(jnp.int32, (1, 8, 1), 1)
+
+        def cells(comp, dy):
+            return vs[t, comp, 1 + dy:13 + dy]
 
         def slope_x(comp):
-            return (cells(comp, 1, 0) - cells(comp, -1, 0)) * 0.5
+            here = cells(comp, 0)
+            above = jnp.where(x_cell == 7, xs[t, 1, comp - 1], roll(here, -1, 1))
+            below = jnp.where(x_cell == 0, xs[t, 0, comp - 1], roll(here, 1, 1))
+            return (above - below) * 0.5
 
         def slope_y(comp):
-            return (cells(comp, 0, 1) - cells(comp, 0, -1)) * 0.5
+            return (cells(comp, 1) - cells(comp, -1)) * 0.5
 
         def slope_z(comp):
-            here = cells(comp, 0, 0)
+            here = cells(comp, 0)
             return (roll(here, -1, 2) - roll(here, 1, 2)) * 0.5
 
         curl_x = slope_y(2) - slope_z(1)
         curl_y = slope_z(0) - slope_x(2)
         curl_z = slope_x(1) - slope_y(0)
-        v_x, v_y, v_z = cells(0, 0, 0), cells(1, 0, 0), cells(2, 0, 0)
+        v_x, v_y, v_z = cells(0, 0), cells(1, 0), cells(2, 0)
         lamb = (curl_y * v_z - curl_z * v_y, curl_z * v_x - curl_x * v_z, curl_x * v_y - curl_y * v_x)
         for comp in range(3):
             for side in range(2):
-                lr[side, :, comp * 12:comp * 12 + 12, :] = lamb[comp][:, :12, side * 128:side * 128 + 128]
+                lr[side, comp * 96:comp * 96 + 96, :] = lamb[comp][:, :, side * 128:side * 128 + 128].reshape(96, 128)
         columns = []
         for row in range(4):
-            low = swap_chunks(lr[0, :, pl.ds(row, 16, stride=4), :])
-            high = swap_chunks(lr[1, :, pl.ds(row, 16, stride=4), :])
+            low, high = (
+                swap_chunks(jnp.stack(
+                    [lr[side, pl.ds(row * 8 + at, 16, stride=32), :] for at in range(8)]))
+                for side in range(2))
             columns.append(jnp.concatenate([low, high[:4]], axis=0))
         cut = jnp.concatenate(columns, axis=2).reshape(192, 512).astype(BF16)
         made = jnp.dot(cut, ip[...].reshape(512, 512), preferred_element_type=F32).astype(BF16)
@@ -457,11 +477,13 @@
             for part in range(4):
                 forc[t, comp, part] = placed[comp * 32:comp * 32 + 32, part * 128:part * 128 + 128]
 
-    def put_sources(t):
-        table = recvb[t].reshape(n_dev * ROWS, 512)
-        chosen = jnp.dot(choose, table, preferred_element_type=F32).astype(BF16)
+    def put_sources():
+        chosen = [
+            jnp.dot(choose, recvb[t].reshape(n_dev * ROWS, 512), preferred_element_type=F32)
+            for t in range(2)]
         for comp in range(3):
-            out_s[t * 3 + comp] = chosen[comp * count:comp * count + count]
+            rows = slice(comp * count, comp * count + count)
+            out_s[:, comp] = jnp.stack([chosen[0][rows], chosen[1][rows]], axis=1).astype(BF16)
 
     for at in range(4):
         loads[3 + at].wait()
@@ -482,7 +504,6 @@
     advance_local(1, 0, 0)
     put_faces(2)
     send_faces(2)
-    put_sources(0)
     take_faces(1)
     add_neighbours(1, False)
     send_edges(2)
@@ -500,7 +521,7 @@
     advance_local(3, 3, 1)
     put_faces(4)
     send_faces(4)
-    put_sources(1)
+    put_sources()
     take_faces(3)
     take_edges(2)
     add_neighbours(3, True)
@@ -548,30 +569,46 @@
                 diagonal(k, at, x_at[1 - way_x], y_at[1 - way_y]).wait_send()
 
 
+def finish(q_in, s_in, q_out, s_out, sems):
+    copies = [
+        pltpu.make_async_copy(q_in, q_out, sems.at[0]),
+        pltpu.make_async_copy(s_in, s_out, sems.at[1]),
+    ]
+    for copy in copies:
+        copy.start()
+    for copy in copies:
+        copy.wait()
+
+
 def body(n_sec, n_dev, velocity, acoustic, interp, source_peer, source_block, source_element):
     count = source_peer.shape[0]
     wtab, coef = tables()
-    any_spec = pl.BlockSpec(memory_space=pltpu.HBM)
+    hbm = pl.BlockSpec(memory_space=pltpu.HBM)
     vmem = pl.BlockSpec(memory_space=pltpu.VMEM)
     dma = pltpu.SemaphoreType.DMA
     acoustic_next, sources = pl.pallas_call(
         functools.partial(kernel, n_sec, n_dev),
         out_shape=(
-            jax.ShapeDtypeStruct((4, 32, 512), F32),
-            jax.ShapeDtypeStruct((6, count, 512), BF16),
+            pltpu.VMEM((4, 32, 512), F32),
+            pltpu.VMEM((count, 3, 2, 512), BF16),
         ),
-        in_specs=[any_spec, any_spec, any_spec, vmem, vmem, vmem, any_spec, vmem],
+        in_specs=[hbm] * 8,
         out_specs=(vmem, vmem),
         scratch_shapes=[
-            pltpu.VMEM((2, 3, 8, 12, 192), BF16),
+            pltpu.VMEM((2, 3, 12, 8, 192), BF16),
             pltpu.VMEM((4, 32, 512), F32),
             pltpu.VMEM((4, 8, 16, 512), BF16),
             pltpu.VMEM((2, 256, 256), BF16),
-            pltpu.VMEM((2, 3, 10, 24, 256), F32),
-            pltpu.VMEM((2, 8, 64, 128), F32),
-            pltpu.VMEM((2, 2, 16, 192), BF16),
+            pltpu.VMEM((32, 128), F32),
+            pltpu.VMEM((1, count), jnp.int32),
+            pltpu.VMEM((1, count), jnp.int32),
+            pltpu.VMEM((1, count), jnp.int32),
+            pltpu.VMEM((2, 3, 14, 8, 256), F32),
+            pltpu.VMEM((2, 2, 2, 12, 8, 256), F32),
+            pltpu.VMEM((2, 512, 128), F32),
             pltpu.VMEM((2, 2, 2, 12, 192), BF16),
-            pltpu.VMEM((2, 2, 16, 192), BF16),
+            pltpu.VMEM((2, 2, 2, 12, 192), BF16),
+            pltpu.VMEM((2, 2, 3, 8, 192), BF16),
             pltpu.VMEM((2, 128), F32),
             pltpu.VMEM((n_dev, 2, 128), F32),
             pltpu.VMEM((2, n_dev, ROWS, 512), BF16),
@@ -584,7 +621,7 @@
             pltpu.VMEM((6, 2, 32, 128), BF16),
             pltpu.VMEM((4, 4, 16, 128), BF16),
             pltpu.VMEM((4, 4, 16, 128), BF16),
-            dma((7,)),
+            dma((11,)),
             dma((2, 2)), dma((2, 2)), dma((2, 2)), dma((2, 2)),
             dma((n_dev,)), dma((n_dev,)),
             dma((2, n_dev)), dma((2, n_dev)),
@@ -592,19 +629,29 @@
             dma((4, 4)), dma((4, 4)),
         ],
         compiler_params=pltpu.CompilerParams(
-            collective_id=0, has_side_effects=True, vmem_limit_bytes=40 * 1024 * 1024),
+            collective_id=0, has_side_effects=True, vmem_limit_bytes=66400000),
     )(
-        velocity,
+        velocity.transpose(0, 1, 3, 2, 4),
         acoustic.reshape(4, 32, 512),
         interp.reshape(8, 4, 16, 512),
-        source_peer,
+        source_peer.reshape(1, count),
         source_block.reshape(1, count),
         source_element.reshape(1, count),
         jnp.asarray(wtab),
         jnp.asarray(coef),
     )
-    sources = sources.reshape(2, 3, count, 512).transpose(2, 0, 1, 3)
-    return acoustic_next.reshape(acoustic.shape), sources
+    acoustic_next, sources = pl.pallas_call(
+        finish,
+        out_shape=(
+            jax.ShapeDtypeStruct((4, 32, 512), F32),
+            jax.ShapeDtypeStruct((count, 3, 2, 512), BF16),
+        ),
+        in_specs=[vmem, vmem],
+        out_specs=(hbm, hbm),
+        scratch_shapes=[dma((2,))],
+        compiler_params=pltpu.CompilerParams(vmem_limit_bytes=1024 * 1024),
+    )(acoustic_next, sources)
+    return acoustic_next.reshape(acoustic.shape), sources.transpose(0, 2, 1, 3)
 
 
 def solution(mesh):

time: 41.2 us -> 37 us (0.90)
  local copies, waits for them, and re-layouts: 5.24 us -> 0 us
  Pallas kernels: 35.1 us -> 36.3 us
    unnamed x15 -> x0, local copies, waits for them, and re-layouts: 4.47 us -> none
    pallas_call x1 -> x2, Pallas kernels: 35.1 us -> 36.3 us  [the longest x1 35.5 us: body(): pl.pallas_call(functools.partial(kernel, n_sec, n_dev), out_shape=(pltpu....]
    reshape x1 -> x0, local copies, waits for them, and re-layouts: 0.78 us -> none  [body(): sources = sources.reshape(2, 3, count, 512).transpose(2, 0, 1, 3)]
where the time goes in v1:
time: 37 us; the launch traced here: 36.9 us
  Pallas kernels  36.3 us (98%)
  between operations  0.64 us (2%)
    pallas_call x1, Pallas kernels, body(): pl.pallas_call(functools.partial(kernel, n_sec, n_dev), out_shape=(pltpu....  35.5 us
    pallas_call x1, Pallas kernels, body(): pl.pallas_call(finish, out_shape=(jax.ShapeDtypeStruct((4, 32, 512), F32)...  0.77 us

profile of v1, /device:TPU:1, one launch (start us, length us, event | category | flops | bytes accessed | tf_op | source)
XLA Modules:
  0.0 36.9 jit_solution(12648152961053988534)
XLA Ops:
  0.6 35.5 %shard_map.95 = (f32[4,32,512]{2,1,0:T(8,128)S(1)}, bf16[24,3,2,512]{3,2,1,0:T(2,128)(2,1)S(1)}) custom-call(bf16[2,3,12,8,192]{4,3,2,1,0:T(8,128)(2,1)} %bitcast.11, f32[4,32,512]{2,1,0:T(8,128)} %bitcast.12, bf16[8,4,16,512]{3,2,1,0:T(8,128)(2,1)} %bitcast.10, s32[1,24]{1,0:T(1,128)} %bitcast.13, s32[1,24]{1,0:T(1,128)} %bitcast.14, s32[1,24]{1,0:T(1,128)} %bitcast.15, ...), custom_call_target="tpu_custom_call" | custom-call | tf_op jit(solution)/shard_map/pallas_call | solution.py:589
  36.2 0.8 %shard_map.96 = (f32[4,32,512]{2,1,0:T(8,128)}, bf16[24,3,2,512]{3,2,1,0:T(2,128)(2,1)}) custom-call(f32[4,32,512]{2,1,0:T(8,128)S(1)} %get-tuple-element.6.q_in, bf16[24,3,2,512]{3,2,1,0:T(2,128)(2,1)S(1)} %get-tuple-element.7.s_in), custom_call_target="tpu_custom_call" | custom-call | tf_op jit(solution)/shard_map/pallas_call | solution.py:643
